TPU v7x, 512 devices: a whole 4x8x8 slice. The times are simulated.
512 devices in a mesh: dom: 64 (over z, x, core), col: 8 (over y).
Axes of the slice: x: 4, y: 8, z: 8, core: 2. Of those that a mesh axis runs over, the one named last changes fastest.
Arguments:
- feature: bfloat16 [32768, 1024], P('dom', 'col'), may hold values from -6 to 6
- cotangent: bfloat16 [32768, 1024], P('dom', 'col'), may hold values from -6 to 6
- node_type: int32 [32768], P('dom'), may hold values from 0 to 2
- self_gain: float32 [3, 1024], P(None, 'col'), may hold values from 0.1 to 1.9
- weights: bfloat16 [8, 1024, 1024], P(None, 'dom', 'col'), may hold values from -0.1875 to 0.1875
- tile_values: bfloat16 [2048, 128, 128], P('dom'), may hold values from -0.5 to 0.5
- tile_rel: int32 [2048], P('dom'), may hold values from 0 to 7
- tile_src: int32 [2048], P('dom'), may hold values from 0 to 3
- tile_peer: int32 [2048], P('dom'), may hold values from 0 to 63, as said below
- tile_count: int32 [64], P('dom'), may hold values from 24 to 32, as said below
- send_block: int32 [64, 64], P('dom'), may hold values from -1 to 3, as said below
Outputs:
- feature_grad: bfloat16 [32768, 1024], P('dom', 'col')
- weight_grad: bfloat16 [8, 1024, 1024], P(None, None, 'col')
Inputs may be any that keep to these rules, and one draw needn't show every extreme that they name: Slots 0 to tile_count - 1 of each partition hold its tiles, the others hold none; some partition uses all 32 slots in every draw. `tile_peer`: the used slots of one partition name distinct owner partitions. send_block[o, p] is at least 0 exactly when some used slot of partition p names o, and then it is that slot's destination block within o.
All inputs are finite; a program needn't handle non-finite values.
Results may differ from a plain program's by a relative error of at most 0.0052.
Values may be sent and summed in bfloat16 or wider, within the bound.
No kernel may reach another device: no remote copies, remote signals or barrier semaphores. Data moves between devices by JAX's collectives and lax.ppermute only.
A program may use at most 64 MiB of HBM per device.

v0:
```python
import math
import jax
import jax.numpy as jnp
from jax import lax
from jax.sharding import PartitionSpec as P


def body(
    feature,
    cotangent,
    node_type,
    self_gain,
    weights,
    tile_values,
    tile_rel,
    tile_src,
    tile_peer,
    tile_count,
    send_block,
):
    partitions = lax.axis_size("dom")
    row_count, col_width = cotangent.shape
    tile_size = tile_values.shape[1]
    block_count = row_count // tile_size
    relations = weights.shape[0]
    slot_count = tile_values.shape[0]
    type_count = self_gain.shape[0]
    grad_blocks = cotangent.reshape(block_count, tile_size, col_width)
    wanted = send_block[0]
    chooser = (wanted[:, None] == jnp.arange(block_count, dtype=jnp.int32)[None, :]).astype(
        jnp.bfloat16
    )
    outgoing = jnp.einsum(
        "pb,btk->ptk", chooser, grad_blocks, preferred_element_type=jnp.float32
    ).astype(jnp.bfloat16)
    incoming = lax.all_to_all(outgoing, "dom", split_axis=0, concat_axis=0, tiled=True)
    picked = jnp.take(incoming, tile_peer, axis=0)
    contribs = jnp.einsum("tds,tdk->tsk", tile_values, picked, preferred_element_type=jnp.float32)
    is_used = jnp.arange(slot_count, dtype=jnp.int32) < tile_count[0]
    slot_of = tile_rel * block_count + tile_src
    slot_table = (
        (slot_of[None, :] == jnp.arange(relations * block_count, dtype=jnp.int32)[:, None])
        & is_used[None, :]
    ).astype(jnp.float32)
    merged = jnp.einsum("mt,tsk->msk", slot_table, contribs, precision=lax.Precision.HIGHEST)
    block_grad = merged.astype(jnp.bfloat16).reshape(relations, row_count, col_width)
    kind_table = (node_type[:, None] == jnp.arange(type_count, dtype=jnp.int32)[None, :]).astype(
        jnp.float32
    )
    self_gains = jnp.dot(kind_table, self_gain, precision=lax.Precision.HIGHEST)
    self_term = cotangent.astype(jnp.float32) * self_gains
    weight_full = lax.all_gather(weights, "dom", axis=1, tiled=True)
    weight_cols = lax.all_to_all(weight_full, "col", split_axis=1, concat_axis=2, tiled=True)
    aggregated = jnp.einsum(
        "rnk,rjk->nj",
        lax.all_gather(block_grad, "col", axis=2, tiled=True),
        weight_cols,
        preferred_element_type=jnp.float32,
    )
    feature_grad = (aggregated + self_term).astype(jnp.bfloat16)
    weight_terms = jnp.einsum(
        "nj,rnk->rjk",
        lax.all_gather(feature, "col", axis=1, tiled=True),
        block_grad,
        preferred_element_type=jnp.float32,
    )
    norm_scale = 1.0 / math.sqrt(row_count * partitions)
    summed = lax.psum(weight_terms, "dom")
    weight_grad = (summed * norm_scale).astype(jnp.bfloat16)
    return (feature_grad, weight_grad)


def solution(mesh):
    return jax.shard_map(
        body,
        mesh=mesh,
        in_specs=(
            P("dom", "col"),
            P("dom", "col"),
            P("dom"),
            P(None, "col"),
            P(None, "dom", "col"),
            P("dom", None, None),
            P("dom"),
            P("dom"),
            P("dom"),
            P("dom"),
            P("dom", None),
        ),
        out_specs=(P("dom", "col"), P(None, None, "col")),
        check_vma=False,
    )
```

profile of v0, /device:TPU:2, one launch (start us, length us, event | category | flops | bytes accessed | tf_op | source)
XLA Modules:
  0.0 470.0 jit_solution(14236573666321858946)
XLA Ops:
  7.2 0.0 copy-start
  7.2 0.0 all-gather.8.cloned.1.call-start
  7.2 0.7 all-gather.8.cloned.1.call-update
  7.9 1.7 convolution_convert_fusion
  9.6 2.7 copy.38
  12.3 0.0 copy-start.3
  12.3 0.0 copy-start.6
  12.3 0.0 copy-start.7
  12.3 0.0 copy-start.8
  12.3 14.0 %all-to-all-start = ((bf16[64,128,128]{2,1,0:T(8,128)(2,1)}), bf16[64,128,128]{2,1,0:T(8,128)(2,1)S(1)}, u32[]{:S(2)}, u32[]{:S(2)}) async-start(bf16[64,128,128]{2,1,0:T(8,128)(2,1)} %copy.38), calls=%async_computation | async-start | bytes 4194304 | tf_op jit(solution)/shard_map/all_to_all | solution.py:36
  26.3 0.0 all-gather.6.cloned.1.call-start
  26.4 0.0 copy-done.3
  26.4 0.6 copy.42
  27.0 0.1 all-gather.6.cloned.1.call-update
  27.1 0.0 all-reduce.2.cloned.1.call-start
  27.8 0.0 copy-done.6
  27.8 0.0 copy-done.7
  27.8 0.0 copy-done.8
  27.8 49.7 %all-to-all-done = bf16[64,128,128]{2,1,0:T(8,128)(2,1)S(1)} async-done(((bf16[64,128,128]{2,1,0:T(8,128)(2,1)}), bf16[64,128,128]{2,1,0:T(8,128)(2,1)S(1)}, u32[]{:S(2)}, u32[]{:S(2)}) %all-to-all-start) | async-done | bytes 2097184 | tf_op jit(solution)/shard_map/all_to_all | solution.py:36
  77.6 1.7 gather_fusion
  79.2 0.0 copy-done
  79.3 3.1 convolution_bitcast_fusion.1
  82.4 2.4 copy.40
  84.8 1.1 convolution_convert_fusion.1
  85.9 0.4 copy.41
  86.3 0.0 copy-start.1
  86.3 0.0 all-gather.8.cloned.1.call-done
  86.4 4.8 %convolution_bitcast_fusion = f32[8,1024,128]{1,2,0:T(8,128)} fusion(bf16[8,512,128]{2,1,0:T(8,128)(2,1)S(1)} %bitcast.32, bf16[512,1024]{1,0:T(8,128)(2,1)} %all-gather.8.cloned.1.call-done), kind=kOutput, calls=%fused_computation.2 | convolution fusion | flops 1073741824 | bytes 6291456 | tf_op jit(solution)/shard_map/nj,rnk->rjk/dot_general | solution.py:61
  91.2 0.0 copy-done.1
  91.2 0.0 all-reduce.2.cloned.1.call-update
  91.2 0.0 all-gather.4.cloned.1.call-start
  91.3 0.5 all-gather.4.cloned.1.call-update
  91.8 50.8 %all-gather.6.cloned.1.call-done = bf16[8,1024,128]{2,0,1:T(8,128)(2,1)} async-done(((bf16[8,16,128]{2,0,1:T(8,128)(2,1)}), bf16[8,1024,128]{2,0,1:T(8,128)(2,1)}) %all-gather.6.cloned.1.call-update) | async-done | bytes 2097168 | tf_op jit(solution)/shard_map/all_gather | solution.py:52
  142.7 6.7 %all-to-all-start.1 = ((bf16[8,1024,128]{2,0,1:T(8,128)(2,1)}), bf16[8,1024,128]{2,0,1:T(8,128)(2,1)}, u32[]{:S(2)}, u32[]{:S(2)}) async-start(bf16[8,1024,128]{2,0,1:T(8,128)(2,1)} %all-gather.6.cloned.1.call-done), calls=%async_computation.1 | async-start | bytes 4194304 | tf_op jit(solution)/shard_map/all_to_all | solution.py:53
  149.4 202.8 %all-reduce.2.cloned.1.call-done = f32[8,1024,128]{1,2,0:T(8,128)} async-done(((f32[8,1024,128]{1,2,0:T(8,128)}), f32[8,1024,128]{1,2,0:T(8,128)}) %all-reduce.2.cloned.1.call-update) | async-done | bytes 4194320 | tf_op jit(solution)/shard_map/psum | solution.py:68
  352.2 2.8 multiply_convert_fusion
  355.0 2.4 copy.45
  357.4 0.0 all-to-all-done.1
  357.4 2.9 copy.51
  360.3 2.4 all_to_all.20
  362.7 0.0 copy-start.2
  362.7 0.0 copy-start.4
  362.7 93.4 %all-gather.4.cloned.1.call-done = bf16[8,512,1024]{2,1,0:T(8,128)(2,1)} async-done(((bf16[8,512,128]{2,1,0:T(8,128)(2,1)}), bf16[8,512,1024]{2,1,0:T(8,128)(2,1)}) %all-gather.4.cloned.1.call-update) | async-done | bytes 8388624 | tf_op jit(solution)/shard_map/all_gather | solution.py:56
  456.2 6.3 %convolution_bitcast_fusion.2 = f32[512,128]{1,0:T(8,128)S(1)} fusion(bf16[8,512,1024]{2,1,0:T(8,128)(2,1)} %all-gather.4.cloned.1.call-done, bf16[8,128,1024]{2,1,0:T(8,128)(2,1)} %all_to_all.20), kind=kOutput, calls=%fused_computation.9 | convolution fusion | flops 1073741824 | bytes 10747904 | tf_op jit(solution)/shard_map/rnk,rjk->nj/dot_general | solution.py:54
  462.5 0.0 copy-done.2
  462.5 0.0 copy-done.4
  462.5 0.0 copy-done.5
  462.5 1.0 fusion.1
  (6 shorter events, 0.0 us)
Async XLA Ops:
  7.2 72.1 %copy-start = (bf16[32,128,128]{2,1,0:T(8,128)(2,1)S(1)}, bf16[32,128,128]{2,1,0:T(8,128)(2,1)}, u32[]{:S(2)}) copy-start(bf16[32,128,128]{2,1,0:T(8,128)(2,1)} %param.16) | copy-start | bytes 3145732
  7.2 79.2 %all-gather.8.cloned.1.call-start = ((), (), s32[]{:S(2)}) async-start(), calls=%async_computation.4 | async-start | bytes 1179648 | tf_op jit(solution)/shard_map/all_gather | solution.py:63
  12.3 14.1 %copy-start.3 = (bf16[8,16,128]{2,1,0:T(8,128)(2,1)S(1)}, bf16[8,16,128]{2,1,0:T(8,128)(2,1)}, u32[]{:S(2)}) copy-start(bf16[8,16,128]{2,1,0:T(8,128)(2,1)} %param.15) | copy-start | bytes 98308
  12.3 15.5 %copy-start.6 = (s32[32]{0:T(128)S(1)}, s32[32]{0:T(128)}, u32[]{:S(2)}) copy-start(s32[32]{0:T(128)} %param.19) | copy-start | bytes 388
  12.3 15.5 %copy-start.7 = (s32[32]{0:T(128)S(1)}, s32[32]{0:T(128)}, u32[]{:S(2)}) copy-start(s32[32]{0:T(128)} %param.18) | copy-start | bytes 388
  12.3 15.5 %copy-start.8 = (s32[32]{0:T(128)S(1)}, s32[32]{0:T(128)}, u32[]{:S(2)}) copy-start(s32[32]{0:T(128)} %param.17) | copy-start | bytes 388
  12.3 65.3 %all-to-all-start = ((bf16[64,128,128]{2,1,0:T(8,128)(2,1)}), bf16[64,128,128]{2,1,0:T(8,128)(2,1)S(1)}, u32[]{:S(2)}, u32[]{:S(2)}) async-start(bf16[64,128,128]{2,1,0:T(8,128)(2,1)} %copy.38), calls=%async_computation | async-start | bytes 4194304 | tf_op jit(solution)/shard_map/all_to_all | solution.py:36
  26.3 116.4 %all-gather.6.cloned.1.call-start = ((), (), s32[]{:S(2)}) async-start(), calls=%async_computation.3 | async-start | bytes 2129920 | tf_op jit(solution)/shard_map/all_gather | solution.py:52
  27.1 325.2 %all-reduce.2.cloned.1.call-start = ((), (), s32[]{:S(2)}) async-start(), calls=%async_computation.5 | async-start | bytes 8388608 | tf_op jit(solution)/shard_map/psum | solution.py:68
  86.3 4.9 %copy-start.1 = (bf16[32,128,128]{2,1,0:T(8,128)(2,1)}, bf16[32,128,128]{2,1,0:T(8,128)(2,1)S(1)}, u32[]{:S(2)}) copy-start(bf16[32,128,128]{2,1,0:T(8,128)(2,1)S(1)} %copy.41) | copy-start | bytes 3145732
  91.2 364.9 %all-gather.4.cloned.1.call-start = ((), (), s32[]{:S(2)}) async-start(), calls=%async_computation.2 | async-start | bytes 9437184 | tf_op jit(solution)/shard_map/all_gather | solution.py:56
  142.7 214.7 %all-to-all-start.1 = ((bf16[8,1024,128]{2,0,1:T(8,128)(2,1)}), bf16[8,1024,128]{2,0,1:T(8,128)(2,1)}, u32[]{:S(2)}, u32[]{:S(2)}) async-start(bf16[8,1024,128]{2,0,1:T(8,128)(2,1)} %all-gather.6.cloned.1.call-done), calls=%async_computation.1 | async-start | bytes 4194304 | tf_op jit(solution)/shard_map/all_to_all | solution.py:53
  362.7 99.8 %copy-start.2 = (bf16[512,128]{1,0:T(8,128)(2,1)S(1)}, bf16[512,128]{1,0:T(8,128)(2,1)}, u32[]{:S(2)}) copy-start(bf16[512,128]{1,0:T(8,128)(2,1)} %param.12) | copy-start | bytes 393220
  362.7 99.8 %copy-start.4 = (f32[3,128]{1,0:T(4,128)S(1)}, f32[3,128]{1,0:T(4,128)}, u32[]{:S(2)}) copy-start(f32[3,128]{1,0:T(4,128)} %param.14) | copy-start | bytes 4612
  362.7 99.8 %copy-start.5 = (s32[512]{0:T(512)S(1)}, s32[512]{0:T(512)}, u32[]{:S(2)}) copy-start(s32[512]{0:T(512)} %param.13) | copy-start | bytes 6148
Sparse Core Ops, SparseCore 0:
  10.0 46.7 all-gather.7
  60.7 81.9 all-gather.5
  146.2 205.9 all-reduce.1
  354.3 101.8 all-gather.3
where the time goes:
time: 471 us; the launch traced here: 470 us
  waiting for transfers between devices  398 us (85%)
  starting transfers between devices  20.9 us (4%)
  matrix products  18.1 us (4%)
  local copies, waits for them, and re-layouts  15.5 us (3%)
  between operations  14.6 us (3%)
    psum x1, waiting for transfers between devices, body(): summed = lax.psum(weight_terms, 'dom')  203 us
    all_gather x1, waiting for transfers between devices, body(): lax.all_gather(block_grad, 'col', axis=2, tiled=True)  93.4 us
    all_gather x1, waiting for transfers between devices, body(): weight_full = lax.all_gather(weights, 'dom', axis=1, tiled=True)  50.8 us
    all_to_all x1, waiting for transfers between devices, body(): lax.all_to_all(outgoing, 'dom', split_axis=0, concat_axis=0, tiled=True)  49.7 us
    all_to_all x1, starting transfers between devices, body(): lax.all_to_all(outgoing, 'dom', split_axis=0, concat_axis=0, tiled=True)  14 us
  transfers between devices with their start and end apart: 6, of which 4 were waited for; matrix products, arithmetic and copies ran while one was open for 6% of the time, Pallas kernels for 0%

commit v1 on v0

--- a/solution.py
+++ b/solution.py
@@ -51,12 +51,41 @@
     self_term = cotangent.astype(jnp.float32) * self_gains
     weight_full = lax.all_gather(weights, "dom", axis=1, tiled=True)
     weight_cols = lax.all_to_all(weight_full, "col", split_axis=1, concat_axis=2, tiled=True)
+    mixed_arr, top, opened = (
+        jax.lax.axis_size("col"),
+        jax.lax.axis_index("col"),
+        block_grad.shape[2],
+    )
+    chunks = [(tick, (tick + 1) % mixed_arr) for tick in range(mixed_arr)]
+    items = [(tick, (tick - 1) % mixed_arr) for tick in range(mixed_arr)]
+    mat_out = mixed_arr // 2
+    local_next = passed = block_grad
     aggregated = jnp.einsum(
         "rnk,rjk->nj",
-        lax.all_gather(block_grad, "col", axis=2, tiled=True),
-        weight_cols,
+        block_grad,
+        lax.dynamic_slice_in_dim(weight_cols, top * opened, block_grad.shape[2], axis=2),
         preferred_element_type=jnp.float32,
     )
+    for i0 in [*range(1, mat_out + 1)]:
+        local_next = jax.lax.ppermute(local_next, "col", chunks)
+        if i0 < mixed_arr - mat_out:
+            passed = jax.lax.ppermute(passed, "col", items)
+            aggregated = aggregated + jnp.einsum(
+                "rnk,rjk->nj",
+                passed,
+                lax.dynamic_slice_in_dim(
+                    weight_cols, (top + i0) % mixed_arr * opened, passed.shape[2], axis=2
+                ),
+                preferred_element_type=jnp.float32,
+            )
+        aggregated = aggregated + jnp.einsum(
+            "rnk,rjk->nj",
+            local_next,
+            lax.dynamic_slice_in_dim(
+                weight_cols, (top - i0) % mixed_arr * opened, local_next.shape[2], axis=2
+            ),
+            preferred_element_type=jnp.float32,
+        )
     feature_grad = (aggregated + self_term).astype(jnp.bfloat16)
     weight_terms = jnp.einsum(
         "nj,rnk->rjk",

time: 471 us -> 438 us (0.930)
  waiting for transfers between devices: 398 us -> 326 us
  starting transfers between devices: 20.9 us -> 45.6 us
  local copies, waits for them, and re-layouts: 15.5 us -> 22.4 us
  matrix products: 18.1 us -> 23.9 us
    all_gather x1 -> x0, waiting for transfers between devices: 93.4 us -> none  [body(): lax.all_gather(block_grad, 'col', axis=2, tiled=True)]
    all_gather x1, waiting for transfers between devices: 0.02 us -> 50.7 us  [body(): lax.all_gather(feature, 'col', axis=1, tiled=True)]
    all_to_all x1, waiting for transfers between devices: 49.7 us -> 0.01 us  [body(): lax.all_to_all(outgoing, 'dom', split_axis=0, concat_axis=0, tiled=True)]
    psum x1, waiting for transfers between devices: 203 us -> 167 us  [body(): summed = lax.psum(weight_terms, 'dom')]
    ppermute x0 -> x7, waiting for transfers between devices: none -> 33 us  [the longest x4 17.7 us: body(): local_next = jax.lax.ppermute(local_next, 'col', chunks)]
    ppermute x0 -> x7, starting transfers between devices: none -> 24.4 us  [the longest x3 14.6 us: body(): passed = jax.lax.ppermute(passed, 'col', items)]
    all_gather x1, waiting for transfers between devices: 50.8 us -> 74.6 us  [body(): weight_full = lax.all_gather(weights, 'dom', axis=1, tiled=True)]
    dot_general x1 -> x8, matrix products: 6.31 us -> 12.7 us  [the longest x4 7.39 us: body(): jnp.einsum('rnk,rjk->nj', local_next, lax.dynamic_slice_in_dim(weight_col...]
  transfers between devices with their start and end apart: 6 -> 12, of which waited for: 4 -> 8; matrix products, arithmetic and copies ran while one was open for 6% -> 10% of each run, Pallas kernels for 0% -> 0%
where the time goes in v1:
time: 438 us; the launch traced here: 437 us
  waiting for transfers between devices  326 us (74%)
  starting transfers between devices  45.6 us (10%)
  matrix products  23.9 us (5%)
  local copies, waits for them, and re-layouts  22.4 us (5%)
  between operations  14.8 us (3%)
    psum x1, waiting for transfers between devices, body(): summed = lax.psum(weight_terms, 'dom')  167 us
    all_gather x1, waiting for transfers between devices, body(): weight_full = lax.all_gather(weights, 'dom', axis=1, tiled=True)  74.6 us
    all_gather x1, waiting for transfers between devices, body(): lax.all_gather(feature, 'col', axis=1, tiled=True)  50.7 us
    ppermute x4, waiting for transfers between devices, body(): local_next = jax.lax.ppermute(local_next, 'col', chunks)  17.7 us
    ppermute x3, waiting for transfers between devices, body(): passed = jax.lax.ppermute(passed, 'col', items)  15.3 us
    ppermute x3, starting transfers between devices, body(): passed = jax.lax.ppermute(passed, 'col', items)  14.6 us
    all_to_all x1, starting transfers between devices, body(): lax.all_to_all(outgoing, 'dom', split_axis=0, concat_axis=0, tiled=True)  14.2 us
    ppermute x4, starting transfers between devices, body(): local_next = jax.lax.ppermute(local_next, 'col', chunks)  9.81 us
  transfers between devices with their start and end apart: 12, of which 8 were waited for; matrix products, arithmetic and copies ran while one was open for 10% of the time, Pallas kernels for 0%

profile of v1, /device:TPU:2, one launch (start us, length us, event | category | flops | bytes accessed | tf_op | source)
XLA Modules:
  0.0 437.1 jit_solution(5671091883188988174)
XLA Ops:
  7.2 0.0 copy-start
  7.2 0.0 all-gather.3.cloned.1.call-start
  7.2 1.5 copy.42
  8.7 0.0 all-gather.3.cloned.1.call-update
  8.7 1.7 convolution_convert_fusion
  10.4 2.7 copy.38
  13.1 14.2 %all-to-all-start = ((bf16[64,128,128]{2,1,0:T(8,128)(2,1)}), bf16[64,128,128]{2,1,0:T(8,128)(2,1)}, u32[]{:S(2)}, u32[]{:S(2)}) async-start(bf16[64,128,128]{2,1,0:T(8,128)(2,1)} %copy.38), calls=%async_computation | async-start | bytes 4194304 | tf_op jit(solution)/shard_map/all_to_all | solution.py:36
  27.3 0.0 all-gather.5.cloned.1.call-start
  27.3 0.7 all-gather.5.cloned.1.call-update
  28.8 74.6 %all-gather.3.cloned.1.call-done = bf16[8,1024,128]{2,0,1:T(8,128)(2,1)} async-done(((bf16[8,16,128]{2,0,1:T(8,128)(2,1)}), bf16[8,1024,128]{2,0,1:T(8,128)(2,1)}) %all-gather.3.cloned.1.call-update) | async-done | bytes 2097168 | tf_op jit(solution)/shard_map/all_gather | solution.py:52
  103.4 0.0 all-to-all-done
  103.4 6.9 %all-to-all-start.1 = ((bf16[8,1024,128]{2,0,1:T(8,128)(2,1)}), bf16[8,1024,128]{2,0,1:T(8,128)(2,1)}, u32[]{:S(2)}, u32[]{:S(2)}) async-start(bf16[8,1024,128]{2,0,1:T(8,128)(2,1)} %all-gather.3.cloned.1.call-done), calls=%async_computation.1 | async-start | bytes 4194304 | tf_op jit(solution)/shard_map/all_to_all | solution.py:53
  110.3 0.0 all-reduce.2.cloned.1.call-start
  110.3 2.3 gather_fusion
  112.7 1.9 convolution_bitcast_fusion.1
  114.6 3.1 copy.40
  117.7 2.7 convolution_convert_fusion.1
  120.4 0.4 copy.41
  120.8 3.9 collective-permute-start.1
  124.7 50.7 %all-gather.5.cloned.1.call-done = bf16[512,1024]{1,0:T(8,128)(2,1)} async-done(((bf16[512,128]{1,0:T(8,128)(2,1)}), bf16[512,1024]{1,0:T(8,128)(2,1)}) %all-gather.5.cloned.1.call-update) | async-done | bytes 1048592 | tf_op jit(solution)/shard_map/all_gather | solution.py:92
  175.4 4.5 %convolution_bitcast_fusion = f32[8,1024,128]{1,2,0:T(8,128)} fusion(bf16[8,512,128]{2,1,0:T(8,128)(2,1)S(1)} %bitcast.71, bf16[512,1024]{1,0:T(8,128)(2,1)} %all-gather.5.cloned.1.call-done), kind=kOutput, calls=%fused_computation.2 | convolution fusion | flops 1073741824 | bytes 6291456 | tf_op jit(solution)/shard_map/nj,rnk->rjk/dot_general | solution.py:90
  179.9 0.0 all-reduce.2.cloned.1.call-update
  180.0 4.3 collective-permute-start
  184.3 7.3 %collective-permute-done.1 = bf16[8,512,128]{2,1,0:T(8,128)(2,1)} collective-permute-done((bf16[8,512,128]{2,1,0:T(8,128)(2,1)S(1)}, bf16[8,512,128]{2,1,0:T(8,128)(2,1)}, u32[]{:S(2)}, u32[]{:S(2)}) %collective-permute-start.1) | collective-permute-done | bytes 1048608 | tf_op jit(solution)/shard_map/ppermute | solution.py:70
  191.6 1.9 collective-permute-start.3
  193.5 13.4 %collective-permute-done = bf16[8,512,128]{2,1,0:T(8,128)(2,1)S(1)} collective-permute-done((bf16[8,512,128]{2,1,0:T(8,128)(2,1)S(1)}, bf16[8,512,128]{2,1,0:T(8,128)(2,1)S(1)}, u32[]{:S(2)}, u32[]{:S(2)}) %collective-permute-start) | collective-permute-done | bytes 1048608 | tf_op jit(solution)/shard_map/ppermute | solution.py:72
  206.9 5.6 %collective-permute-start.2 = (bf16[8,512,128]{2,1,0:T(8,128)(2,1)S(1)}, bf16[8,512,128]{2,1,0:T(8,128)(2,1)}, u32[]{:S(2)}, u32[]{:S(2)}) collective-permute-start(bf16[8,512,128]{2,1,0:T(8,128)(2,1)S(1)} %collective-permute-done), channel_id=1, source_target_pairs={{0,7},{1,0},{2,1},{3,2},{4,3},{5,4},{6,5},{7,6},{8,15},{9,8},{10,9... | collective-permute-start | bytes 3145736 | tf_op jit(solution)/shard_map/ppermute | solution.py:72
  212.5 6.7 %collective-permute-done.3 = bf16[8,512,128]{2,1,0:T(8,128)(2,1)} collective-permute-done((bf16[8,512,128]{2,1,0:T(8,128)(2,1)}, bf16[8,512,128]{2,1,0:T(8,128)(2,1)}, u32[]{:S(2)}, u32[]{:S(2)}) %collective-permute-start.3) | collective-permute-done | bytes 1048608 | tf_op jit(solution)/shard_map/ppermute | solution.py:70
  219.2 1.9 collective-permute-start.5
  221.3 0.3 convolution_multiply_fusion
  221.6 167.2 %all-reduce.2.cloned.1.call-done = f32[8,1024,128]{1,2,0:T(8,128)} async-done(((f32[8,1024,128]{1,2,0:T(8,128)}), f32[8,1024,128]{1,2,0:T(8,128)}) %all-reduce.2.cloned.1.call-update) | async-done | bytes 4194320 | tf_op jit(solution)/shard_map/psum | solution.py:97
  388.9 4.1 multiply_convert_fusion
  393.0 3.9 copy.45
  396.9 0.0 collective-permute-done.2
  396.9 4.7 %collective-permute-start.4 = (bf16[8,512,128]{2,1,0:T(8,128)(2,1)}, bf16[8,512,128]{2,1,0:T(8,128)(2,1)}, u32[]{:S(2)}, u32[]{:S(2)}) collective-permute-start(bf16[8,512,128]{2,1,0:T(8,128)(2,1)} %collective-permute-done.2), channel_id=1, source_target_pairs={{0,7},{1,0},{2,1},{3,2},{4,3},{5,4},{6,5},{7,6},{8,15},{9,8},{10,9... | collective-permute-start | bytes 3145736 | tf_op jit(solution)/shard_map/ppermute | solution.py:72
  401.6 2.1 collective-permute-start.6
  403.8 4.3 copy.51
  408.0 4.1 all_to_all.20
  412.2 1.5 convolution_bitcast_fusion.9
  413.7 1.7 convolution_bitcast_fusion.7
  415.4 1.7 convolution_bitcast_fusion.5
  417.1 1.7 convolution_bitcast_fusion.3
  418.8 0.5 fusion.1
  419.3 1.7 fusion.3
  421.0 1.9 collective-permute-done.4
  422.9 1.7 fusion.5
  424.6 3.7 collective-permute-done.6
  428.2 2.3 fusion.8
  (22 shorter events, 0.1 us)
Async XLA Ops:
  7.2 105.5 %copy-start = (bf16[32,128,128]{2,1,0:T(8,128)(2,1)S(1)}, bf16[32,128,128]{2,1,0:T(8,128)(2,1)}, u32[]{:S(2)}) copy-start(bf16[32,128,128]{2,1,0:T(8,128)(2,1)} %param.16) | copy-start | bytes 3145732
  7.2 96.2 %all-gather.3.cloned.1.call-start = ((), (), s32[]{:S(2)}) async-start(), calls=%async_computation.2 | async-start | bytes 2129920 | tf_op jit(solution)/shard_map/all_gather | solution.py:52
  13.1 15.6 %copy-start.5 = (s32[32]{0:T(128)S(1)}, s32[32]{0:T(128)}, u32[]{:S(2)}) copy-start(s32[32]{0:T(128)} %param.19) | copy-start | bytes 388
  13.1 15.7 %copy-start.6 = (s32[32]{0:T(128)S(1)}, s32[32]{0:T(128)}, u32[]{:S(2)}) copy-start(s32[32]{0:T(128)} %param.18) | copy-start | bytes 388
  13.1 15.7 %copy-start.7 = (s32[32]{0:T(128)S(1)}, s32[32]{0:T(128)}, u32[]{:S(2)}) copy-start(s32[32]{0:T(128)} %param.17) | copy-start | bytes 388
  13.1 90.3 %all-to-all-start = ((bf16[64,128,128]{2,1,0:T(8,128)(2,1)}), bf16[64,128,128]{2,1,0:T(8,128)(2,1)}, u32[]{:S(2)}, u32[]{:S(2)}) async-start(bf16[64,128,128]{2,1,0:T(8,128)(2,1)} %copy.38), calls=%async_computation | async-start | bytes 4194304 | tf_op jit(solution)/shard_map/all_to_all | solution.py:36
  27.3 148.1 %all-gather.5.cloned.1.call-start = ((), (), s32[]{:S(2)}) async-start(), calls=%async_computation.3 | async-start | bytes 1179648 | tf_op jit(solution)/shard_map/all_gather | solution.py:92
  103.4 300.4 %all-to-all-start.1 = ((bf16[8,1024,128]{2,0,1:T(8,128)(2,1)}), bf16[8,1024,128]{2,0,1:T(8,128)(2,1)}, u32[]{:S(2)}, u32[]{:S(2)}) async-start(bf16[8,1024,128]{2,0,1:T(8,128)(2,1)} %all-gather.3.cloned.1.call-done), calls=%async_computation.1 | async-start | bytes 4194304 | tf_op jit(solution)/shard_map/all_to_all | solution.py:53
  110.3 278.6 %all-reduce.2.cloned.1.call-start = ((), (), s32[]{:S(2)}) async-start(), calls=%async_computation.4 | async-start | bytes 8388608 | tf_op jit(solution)/shard_map/psum | solution.py:97
  120.8 70.8 %collective-permute-start.1 = (bf16[8,512,128]{2,1,0:T(8,128)(2,1)S(1)}, bf16[8,512,128]{2,1,0:T(8,128)(2,1)}, u32[]{:S(2)}, u32[]{:S(2)}) collective-permute-start(bf16[8,512,128]{2,1,0:T(8,128)(2,1)S(1)} %bitcast.70), channel_id=1, source_target_pairs={{0,1},{1,2},{2,3},{3,4},{4,5},{5,6},{6,7},{7,0},{8,9},{9,10},{10,1... | collective-permute-start | bytes 3145736 | tf_op jit(solution)/shard_map/ppermute | solution.py:70
  179.9 41.3 %copy-start.2 = (bf16[512,128]{1,0:T(8,128)(2,1)S(1)}, bf16[512,128]{1,0:T(8,128)(2,1)}, u32[]{:S(2)}) copy-start(bf16[512,128]{1,0:T(8,128)(2,1)} %param.12) | copy-start | bytes 393220
  179.9 41.3 %copy-start.3 = (f32[3,128]{1,0:T(4,128)S(1)}, f32[3,128]{1,0:T(4,128)}, u32[]{:S(2)}) copy-start(f32[3,128]{1,0:T(4,128)} %param.14) | copy-start | bytes 4612
  179.9 41.4 %copy-start.4 = (s32[512]{0:T(512)S(1)}, s32[512]{0:T(512)}, u32[]{:S(2)}) copy-start(s32[512]{0:T(512)} %param.13) | copy-start | bytes 6148
  180.0 26.9 %collective-permute-start = (bf16[8,512,128]{2,1,0:T(8,128)(2,1)S(1)}, bf16[8,512,128]{2,1,0:T(8,128)(2,1)S(1)}, u32[]{:S(2)}, u32[]{:S(2)}) collective-permute-start(bf16[8,512,128]{2,1,0:T(8,128)(2,1)S(1)} %bitcast.72), channel_id=1, source_target_pairs={{0,7},{1,0},{2,1},{3,2},{4,3},{5,4},{6,5},{7,6},{8,15},{9,8},{10,9... | collective-permute-start | bytes 3145736 | tf_op jit(solution)/shard_map/ppermute | solution.py:72
  191.6 27.6 %collective-permute-start.3 = (bf16[8,512,128]{2,1,0:T(8,128)(2,1)}, bf16[8,512,128]{2,1,0:T(8,128)(2,1)}, u32[]{:S(2)}, u32[]{:S(2)}) collective-permute-start(bf16[8,512,128]{2,1,0:T(8,128)(2,1)} %collective-permute-done.1), channel_id=1, source_target_pairs={{0,1},{1,2},{2,3},{3,4},{4,5},{5,6},{6,7},{7,0},{8,9},{9,10},{10,1... | collective-permute-start | bytes 3145736 | tf_op jit(solution)/shard_map/ppermute | solution.py:70
  206.9 190.0 %collective-permute-start.2 = (bf16[8,512,128]{2,1,0:T(8,128)(2,1)S(1)}, bf16[8,512,128]{2,1,0:T(8,128)(2,1)}, u32[]{:S(2)}, u32[]{:S(2)}) collective-permute-start(bf16[8,512,128]{2,1,0:T(8,128)(2,1)S(1)} %collective-permute-done), channel_id=1, source_target_pairs={{0,7},{1,0},{2,1},{3,2},{4,3},{5,4},{6,5},{7,6},{8,15},{9,8},{10,9... | collective-permute-start | bytes 3145736 | tf_op jit(solution)/shard_map/ppermute | solution.py:72
  219.2 182.4 %collective-permute-start.5 = (bf16[8,512,128]{2,1,0:T(8,128)(2,1)}, bf16[8,512,128]{2,1,0:T(8,128)(2,1)}, u32[]{:S(2)}, u32[]{:S(2)}) collective-permute-start(bf16[8,512,128]{2,1,0:T(8,128)(2,1)} %collective-permute-done.3), channel_id=1, source_target_pairs={{0,1},{1,2},{2,3},{3,4},{4,5},{5,6},{6,7},{7,0},{8,9},{9,10},{10,1... | collective-permute-start | bytes 3145736 | tf_op jit(solution)/shard_map/ppermute | solution.py:70
  396.9 26.0 %collective-permute-start.4 = (bf16[8,512,128]{2,1,0:T(8,128)(2,1)}, bf16[8,512,128]{2,1,0:T(8,128)(2,1)}, u32[]{:S(2)}, u32[]{:S(2)}) collective-permute-start(bf16[8,512,128]{2,1,0:T(8,128)(2,1)} %collective-permute-done.2), channel_id=1, source_target_pairs={{0,7},{1,0},{2,1},{3,2},{4,3},{5,4},{6,5},{7,6},{8,15},{9,8},{10,9... | collective-permute-start | bytes 3145736 | tf_op jit(solution)/shard_map/ppermute | solution.py:72
  401.6 26.6 %collective-permute-start.6 = (bf16[8,512,128]{2,1,0:T(8,128)(2,1)}, bf16[8,512,128]{2,1,0:T(8,128)(2,1)}, u32[]{:S(2)}, u32[]{:S(2)}) collective-permute-start(bf16[8,512,128]{2,1,0:T(8,128)(2,1)} %collective-permute-done.5), channel_id=1, source_target_pairs={{0,1},{1,2},{2,3},{3,4},{4,5},{5,6},{6,7},{7,0},{8,9},{9,10},{10,1... | collective-permute-start | bytes 3145736 | tf_op jit(solution)/shard_map/ppermute | solution.py:70
  412.2 3.2 copy-start.1
Sparse Core Ops, SparseCore 0:
  11.9 91.4 all-gather.2
  105.4 69.9 all-gather.4
  180.1 208.7 all-reduce.1
